TPU v7x, 768 devices: a whole 4x8x12 slice. The times are simulated.
768 devices in a mesh: fluid: 2 (over core), zon: 96 (over x, z, y_lo), mer: 4 (over y_hi).
Axes of the slice: x: 4, y: 8 (y_hi: 4, y_lo: 2; y = y_hi * 2 + y_lo), z: 12, core: 2. Of those that a mesh axis runs over, the one named last changes fastest.
Arguments:
- state: float32 [2, 2, 64, 1536, 512], P('fluid', None, None, 'zon', 'mer'), may hold values from -6 to 6
- flow: bfloat16 [2, 2, 64, 1536, 512], P('fluid', None, None, 'zon', 'mer'), may hold values from -0.5 to 0.5
- diffusion: float32 [2, 2, 64], P('fluid'), may hold values from 0.02 to 0.2
- column_solve: float32 [2, 64, 64], P('fluid'), may hold values from -1 to 1, as said below
- exchange_rate: float32 [2, 2], P('fluid'), may hold values from 0.2 to 0.6
- block_map: int32 [16], P('mer'), may hold values from 0 to 15, as said below
- ice_mask: int32 [16], P('mer'), may hold values from 0 to 1
Outputs:
- final_state: float32 [2, 2, 64, 1536, 512], P('fluid', None, None, 'zon', 'mer')
Inputs may be any that keep to these rules, and one draw needn't show every extreme that they name: `column_solve`: entries of the vertical inverses lie within this range; their diagonal is positive. `block_map`: each meridional section of 4 blocks, blocks k * 4 to (k + 1) * 4 - 1, is mapped onto itself by a permutation.
All inputs are finite; a program needn't handle non-finite values.
Results may differ from a plain program's by a relative error of at most 0.0003.
Values may be sent and summed in bfloat16 or wider, within the bound.
A program may use at most 32 MiB of HBM per device.

v0:
```python
import jax
import jax.numpy as jnp
from jax import lax
from jax.sharding import PartitionSpec as P

STEPS = 2


def with_halo(cells, sides, width, closed):
    for axis, dim in sides:
        count = lax.axis_size(axis)
        ends = count if closed else count - 1
        head = lax.slice_in_dim(cells, 0, width, axis=dim)
        tail = lax.slice_in_dim(cells, cells.shape[dim] - width, cells.shape[dim], axis=dim)
        cells = jnp.concatenate(
            [
                lax.ppermute(tail, axis, [(i, (i + 1) % count) for i in range(ends)]),
                cells,
                lax.ppermute(head, axis, [((i + 1) % count, i) for i in range(ends)]),
            ],
            axis=dim,
        )
    return cells


def swapped(block, axis, distance):
    count = lax.axis_size(axis)
    route = []
    for low in range(count):
        high = low | 1 << distance
        if high != low and high < count:
            route += [(low, high), (high, low)]
    return lax.ppermute(block, axis, route)


def advance(
    extended,
    flow_frame,
    viscous,
    vertical,
    coupling,
    local_map,
    inverse,
    open_cols,
    level_pick,
    fluid_id,
):
    padded = with_halo(extended, (("mer", 3),), 1, False)
    centre = padded[:, :, 1:-1, 1:-1]
    east_cell = padded[:, :, 2:, 1:-1]
    west_cell = padded[:, :, :-2, 1:-1]
    north_cell = padded[:, :, 1:-1, 2:]
    south_cell = padded[:, :, 1:-1, :-2]
    levels = centre.shape[1]
    columns = centre.shape[2]
    merid_cols = centre.shape[3]
    block_count = local_map.shape[0]
    block_width = merid_cols // block_count
    own_rows = jnp.where(fluid_id == 0, centre[:, levels - 1], centre[:, 0])
    other_rows = swapped(own_rows, "fluid", 0)
    atm_rows = jnp.where(fluid_id == 0, own_rows, other_rows).reshape(
        -1, columns, block_count, block_width
    )
    ocean_rows = jnp.where(fluid_id == 0, other_rows, own_rows).reshape(
        -1, columns, block_count, block_width
    )
    zonal_flow = flow_frame[0].astype(jnp.float32)
    merid_flow = flow_frame[1].astype(jnp.float32)
    updated = (
        centre
        - 0.5 * zonal_flow * (east_cell - west_cell)
        - 0.5 * merid_flow * (north_cell - south_cell)
        + viscous * (east_cell + west_cell + north_cell + south_cell - 4.0 * centre)
    )
    mapped = jnp.take(atm_rows, local_map, axis=2)
    surface_flux = (mapped - ocean_rows) * open_cols[None, None, :, None]
    returned = jnp.take(surface_flux, inverse, axis=2)
    scaled = coupling[:, None, None, None]
    increment = jnp.where(fluid_id == 0, -scaled * returned, scaled * surface_flux).reshape(
        -1, columns, merid_cols
    )
    updated = updated + level_pick[None, :, None, None] * increment[:, None]
    return jnp.einsum(
        "kl,tlxy->tkxy",
        vertical,
        updated,
        precision=lax.Precision.HIGHEST,
        preferred_element_type=jnp.float32,
    )


def on_device(state, flow, diffusion, column_solve, exchange_rate, block_map, ice_mask):
    tracer_field = state[0]
    flow_local = flow[0]
    levels = tracer_field.shape[1]
    fluid_id = lax.axis_index("fluid")
    block_count = block_map.shape[0]
    local_map = block_map - lax.axis_index("mer") * block_count
    positions = jnp.arange(block_count, dtype=jnp.int32)
    inverse = jnp.sum(
        positions[:, None] * (local_map[:, None] == positions[None, :]).astype(jnp.int32), axis=0
    )
    open_cols = (1 - ice_mask).astype(jnp.float32)
    surface_level = jnp.where(fluid_id == 0, levels - 1, 0).astype(jnp.int32)
    level_pick = (jnp.arange(levels, dtype=jnp.int32) == surface_level).astype(jnp.float32)
    viscous = diffusion[0][:, :, None, None]
    vertical = column_solve[0]
    coupling = exchange_rate[0]
    for step_index in range(STEPS):
        extended = with_halo(tracer_field, (("zon", 2),), 1, True)
        tracer_field = advance(
            extended,
            flow_local,
            viscous,
            vertical,
            coupling,
            local_map,
            inverse,
            open_cols,
            level_pick,
            fluid_id,
        )
    return tracer_field[None]


def solution(mesh):
    return jax.shard_map(
        on_device,
        mesh=mesh,
        in_specs=(
            P("fluid", None, None, "zon", "mer"),
            P("fluid", None, None, "zon", "mer"),
            P("fluid", None, None),
            P("fluid", None, None),
            P("fluid", None),
            P("mer"),
            P("mer"),
        ),
        out_specs=P("fluid", None, None, "zon", "mer"),
        check_vma=False,
    )
```

profile of v0, /device:TPU:48, one launch (start us, length us, event | category | flops | bytes accessed | tf_op | source)
XLA Modules:
  0.0 92.9 jit_solution(987502023642571815)
XLA Ops:
  0.0 1.4 %copy.128 = f32[1,2,64,16,128]{4,3,1,2,0:T(8,128)S(1)} copy(f32[1,2,64,16,128]{4,3,2,1,0:T(8,128)} %param.9) | data formatting | bytes 2097152 | tf_op args[0]
  1.5 1.9 %collective-permute-start.4 = (f32[2,16,128]{2,1,0:T(8,128)S(1)}, f32[2,16,128]{2,1,0:T(8,128)S(1)}, u32[]{:S(2)}, u32[]{:S(2)}) collective-permute-start(f32[2,16,128]{2,1,0:T(8,128)S(1)} %fusion.8), channel_id=1, source_target_pairs={{0,384},{384,0},{1,385},{385,1},{2,386},{386,2},{3,387},{387,3},{4... | collective-permute-start | bytes 49160 | tf_op jit(solution)/shard_map/ppermute | solution.py:33
  3.4 0.1 fusion.12
  3.5 16.9 %collective-permute-start = (f32[2,64,1,128]{3,2,0,1:T(1,128)S(1)}, f32[2,64,1,128]{3,2,0,1:T(1,128)S(1)}, u32[]{:S(2)}, u32[]{:S(2)}) collective-permute-start(f32[2,64,1,128]{3,2,0,1:T(1,128)S(1)} %get-tuple-element.15), channel_id=1, source_target_pairs={{4,0},{8,4},{12,8},{16,12},{20,16},{24,20},{28,24},{32,28},{36,32}... | collective-permute-start | bytes 196616 | tf_op jit(solution)/shard_map/ppermute | solution.py:19
  20.4 1.9 %collective-permute-start.1 = (f32[2,64,1,128]{3,2,0,1:T(1,128)S(1)}, f32[2,64,1,128]{3,2,0,1:T(1,128)S(1)}, u32[]{:S(2)}, u32[]{:S(2)}) collective-permute-start(f32[2,64,1,128]{3,2,0,1:T(1,128)S(1)} %get-tuple-element.14), channel_id=1, source_target_pairs={{0,4},{4,8},{8,12},{12,16},{16,20},{20,24},{24,28},{28,32},{32,36}... | collective-permute-start | bytes 196616 | tf_op jit(solution)/shard_map/ppermute | solution.py:17
  22.5 0.5 compare_and_fusion
  23.1 0.5 bitcast_negate_fusion
  23.6 0.9 multiply_bitcast_fusion.1
  24.5 0.5 compare_convert_fusion
  25.1 0.1 copy.95
  25.4 0.6 gather_fusion
  26.0 0.6 gather_fusion.1
  26.6 4.2 %collective-permute-done.1 = f32[2,64,1,128]{3,2,0,1:T(1,128)S(1)} collective-permute-done((f32[2,64,1,128]{3,2,0,1:T(1,128)S(1)}, f32[2,64,1,128]{3,2,0,1:T(1,128)S(1)}, u32[]{:S(2)}, u32[]{:S(2)}) %collective-permute-start.1) | collective-permute-done | bytes 65568 | tf_op jit(solution)/shard_map/ppermute | solution.py:17
  30.8 0.3 pad_maximum_fusion
  31.1 1.7 %fusion.10 = (f32[2,64,18,1]{3,2,0,1:T(8,128)S(1)}, f32[2,64,18,1]{3,2,0,1:T(8,128)}) fusion(f32[2,64,18,128]{3,2,0,1:T(8,128)S(1)} %pad_maximum_fusion), kind=kLoop, calls=%fused_computation.61 | loop fusion | bytes 36864 | tf_op jit(solution)/shard_map/slice | solution.py:14
  32.8 1.9 %copy.91 = f32[2,64,18,1]{1,0,3,2:T(2,128)S(1)} copy(f32[2,64,18,1]{3,2,0,1:T(8,128)} %get-tuple-element.11) | data formatting | bytes 18432 | tf_op jit(solution)/shard_map/slice | solution.py:13
  34.7 4.0 %collective-permute-start.2 = (f32[2,64,18,1]{1,0,3,2:T(2,128)S(1)}, f32[2,64,18,1]{1,0,3,2:T(2,128)S(1)}, u32[]{:S(2)}, u32[]{:S(2)}) collective-permute-start(f32[2,64,18,1]{1,0,3,2:T(2,128)S(1)} %copy.91), channel_id=1, source_target_pairs={{1,0},{2,1},{3,2},{5,4},{6,5},{7,6},{9,8},{10,9},{11,10},{13,12},{... | collective-permute-start | bytes 27656 | tf_op jit(solution)/shard_map/ppermute | solution.py:19
  38.7 0.5 copy.93
  39.2 1.3 %collective-permute-start.3 = (f32[2,64,18,1]{1,0,3,2:T(2,128)S(1)}, f32[2,64,18,1]{1,0,3,2:T(2,128)S(1)}, u32[]{:S(2)}, u32[]{:S(2)}) collective-permute-start(f32[2,64,18,1]{1,0,3,2:T(2,128)S(1)} %copy.93), channel_id=1, source_target_pairs={{0,1},{1,2},{2,3},{4,5},{5,6},{6,7},{8,9},{9,10},{10,11},{12,13},{... | collective-permute-start | bytes 27656 | tf_op jit(solution)/shard_map/ppermute | solution.py:17
  40.5 0.7 fusion.4
  41.3 0.1 mul.175
  41.5 0.7 copy.92
  42.2 3.6 %collective-permute-done.3 = f32[2,64,18,1]{1,0,3,2:T(2,128)S(1)} collective-permute-done((f32[2,64,18,1]{1,0,3,2:T(2,128)S(1)}, f32[2,64,18,1]{1,0,3,2:T(2,128)S(1)}, u32[]{:S(2)}, u32[]{:S(2)}) %collective-permute-start.3) | collective-permute-done | bytes 9248 | tf_op jit(solution)/shard_map/ppermute | solution.py:17
  45.8 1.8 %copy.94 = f32[2,64,18,1]{3,2,0,1:T(8,128)} copy(f32[2,64,18,1]{1,0,3,2:T(2,128)S(1)} %collective-permute-done.3) | data formatting | bytes 18432 | tf_op jit(solution)/shard_map/ppermute | solution.py:17
  47.6 3.1 %multiply_add_fusion.1 = f32[2,64,16,128]{3,2,0,1:T(8,128)S(1)} fusion(f32[2,64,16,128]{3,2,0,1:T(8,128)S(1)} %bitcast.50, f32[2,64,18,1]{3,2,0,1:T(8,128)S(1)} %copy.92, f32[2,64,1,128]{3,2,0,1:T(1,128)S(1)} %collective-permute-done, f32[2,64,1,128]{3,2,0,1:T(1,128)S(1)} %collective-permute-done.1, f32[2,64,18,1]{3,2,0,1:T(8,128)} %copy.94, ...), kind=kLoop, calls=%fused_computation.28 | loop fusion | flops 6029312 | bytes 3312384 | tf_op jit(solution)/shard_map/add | solution.py:82
  50.7 1.7 %convolution_bitcast_fusion.1 = f32[2,64,16,128]{3,1,2,0:T(8,128)S(1)} fusion(f32[2,64,16,128]{3,2,0,1:T(8,128)S(1)} %multiply_add_fusion.1, f32[1,64,64]{2,1,0:T(8,128)S(1)} %copy-done), kind=kOutput, calls=%fused_computation.7 | convolution fusion | flops 201326592 | bytes 2113536 | tf_op jit(solution)/shard_map/kl,tlxy->tkxy/dot_general | solution.py:83
  52.5 0.6 copy.105
  53.1 1.9 %collective-permute-start.9 = (f32[2,16,128]{2,1,0:T(8,128)S(1)}, f32[2,16,128]{2,1,0:T(8,128)S(1)}, u32[]{:S(2)}, u32[]{:S(2)}) collective-permute-start(f32[2,16,128]{2,1,0:T(8,128)S(1)} %bitcast.51), channel_id=1, source_target_pairs={{0,384},{384,0},{1,385},{385,1},{2,386},{386,2},{3,387},{387,3},{4... | collective-permute-start | bytes 49160 | tf_op jit(solution)/shard_map/ppermute | solution.py:33
  55.0 0.1 fusion.11
  55.1 4.0 %collective-permute-start.5 = (f32[2,64,1,128]{3,2,0,1:T(1,128)S(1)}, f32[2,64,1,128]{3,2,0,1:T(1,128)S(1)}, u32[]{:S(2)}, u32[]{:S(2)}) collective-permute-start(f32[2,64,1,128]{3,2,0,1:T(1,128)S(1)} %get-tuple-element.13), channel_id=1, source_target_pairs={{4,0},{8,4},{12,8},{16,12},{20,16},{24,20},{28,24},{32,28},{36,32}... | collective-permute-start | bytes 196616 | tf_op jit(solution)/shard_map/ppermute | solution.py:19
  59.1 1.9 %collective-permute-start.6 = (f32[2,64,1,128]{3,2,0,1:T(1,128)S(1)}, f32[2,64,1,128]{3,2,0,1:T(1,128)S(1)}, u32[]{:S(2)}, u32[]{:S(2)}) collective-permute-start(f32[2,64,1,128]{3,2,0,1:T(1,128)S(1)} %get-tuple-element.12), channel_id=1, source_target_pairs={{0,4},{4,8},{8,12},{12,16},{16,20},{20,24},{24,28},{28,32},{32,36}... | collective-permute-start | bytes 196616 | tf_op jit(solution)/shard_map/ppermute | solution.py:17
  61.2 0.7 gather_fusion.2
  62.0 0.7 gather_fusion.3
  62.7 6.7 %collective-permute-done.6 = f32[2,64,1,128]{3,2,0,1:T(1,128)S(1)} collective-permute-done((f32[2,64,1,128]{3,2,0,1:T(1,128)S(1)}, f32[2,64,1,128]{3,2,0,1:T(1,128)S(1)}, u32[]{:S(2)}, u32[]{:S(2)}) %collective-permute-start.6) | collective-permute-done | bytes 65568 | tf_op jit(solution)/shard_map/ppermute | solution.py:17
  69.5 0.3 pad_maximum_fusion.1
  69.7 1.7 %fusion.9 = (f32[2,64,18,1]{3,2,0,1:T(8,128)S(1)}, f32[2,64,18,1]{3,2,0,1:T(8,128)}) fusion(f32[2,64,18,128]{3,2,0,1:T(8,128)S(1)} %pad_maximum_fusion.1), kind=kLoop, calls=%fused_computation.60 | loop fusion | bytes 36864 | tf_op jit(solution)/shard_map/slice | solution.py:14
  71.4 1.9 %copy.107 = f32[2,64,18,1]{1,0,3,2:T(2,128)S(1)} copy(f32[2,64,18,1]{3,2,0,1:T(8,128)} %get-tuple-element.9) | data formatting | bytes 18432 | tf_op jit(solution)/shard_map/slice | solution.py:13
  73.3 4.3 %collective-permute-start.7 = (f32[2,64,18,1]{1,0,3,2:T(2,128)S(1)}, f32[2,64,18,1]{1,0,3,2:T(2,128)S(1)}, u32[]{:S(2)}, u32[]{:S(2)}) collective-permute-start(f32[2,64,18,1]{1,0,3,2:T(2,128)S(1)} %copy.107), channel_id=1, source_target_pairs={{1,0},{2,1},{3,2},{5,4},{6,5},{7,6},{9,8},{10,9},{11,10},{13,12},{... | collective-permute-start | bytes 27656 | tf_op jit(solution)/shard_map/ppermute | solution.py:19
  77.7 0.5 copy.109
  78.2 1.5 %collective-permute-start.8 = (f32[2,64,18,1]{1,0,3,2:T(2,128)S(1)}, f32[2,64,18,1]{1,0,3,2:T(2,128)S(1)}, u32[]{:S(2)}, u32[]{:S(2)}) collective-permute-start(f32[2,64,18,1]{1,0,3,2:T(2,128)S(1)} %copy.109), channel_id=1, source_target_pairs={{0,1},{1,2},{2,3},{4,5},{5,6},{6,7},{8,9},{9,10},{10,11},{12,13},{... | collective-permute-start | bytes 27656 | tf_op jit(solution)/shard_map/ppermute | solution.py:17
  79.7 0.7 fusion.2
  80.5 0.1 mul.185
  80.6 0.7 copy.108
  81.3 3.4 %collective-permute-done.8 = f32[2,64,18,1]{1,0,3,2:T(2,128)S(1)} collective-permute-done((f32[2,64,18,1]{1,0,3,2:T(2,128)S(1)}, f32[2,64,18,1]{1,0,3,2:T(2,128)S(1)}, u32[]{:S(2)}, u32[]{:S(2)}) %collective-permute-start.8) | collective-permute-done | bytes 9248 | tf_op jit(solution)/shard_map/ppermute | solution.py:17
  84.7 1.8 %copy.110 = f32[2,64,18,1]{3,2,0,1:T(8,128)} copy(f32[2,64,18,1]{1,0,3,2:T(2,128)S(1)} %collective-permute-done.8) | data formatting | bytes 18432 | tf_op jit(solution)/shard_map/ppermute | solution.py:17
  86.6 3.1 %multiply_add_fusion = f32[2,64,16,128]{3,2,0,1:T(8,128)S(1)} fusion(f32[2,64,16,128]{3,2,0,1:T(8,128)S(1)} %copy.105, f32[2,64,18,1]{3,2,0,1:T(8,128)S(1)} %copy.108, f32[2,64,1,128]{3,2,0,1:T(1,128)S(1)} %collective-permute-done.5, f32[2,64,1,128]{3,2,0,1:T(1,128)S(1)} %collective-permute-done.6, f32[2,64,18,1]{3,2,0,1:T(8,128)} %copy.110, ...), kind=kLoop, calls=%fused_computation.27 | loop fusion | flops 6029312 | bytes 3312384 | tf_op jit(solution)/shard_map/add | solution.py:82
  89.6 1.7 %convolution_bitcast_fusion = f32[1,2,64,16,128]{4,2,3,1,0:T(8,128)S(1)} fusion(f32[2,64,16,128]{3,2,0,1:T(8,128)S(1)} %multiply_add_fusion, f32[1,64,64]{2,1,0:T(8,128)S(1)} %copy-done), kind=kOutput, calls=%fused_computation.6 | convolution fusion | flops 201326592 | bytes 2113536 | tf_op jit(solution)/shard_map/kl,tlxy->tkxy/dot_general | solution.py:83
  91.3 1.6 %copy.118 = f32[1,2,64,16,128]{4,3,2,1,0:T(8,128)} copy(f32[1,2,64,16,128]{4,2,3,1,0:T(8,128)S(1)} %convolution_bitcast_fusion) | data formatting | bytes 2097152 | tf_op jit(solution)/shard_map/broadcast_in_dim | solution.py:123
  (57 shorter events, 0.9 us)
Async XLA Ops:
  0.0 50.7 %copy-start = (f32[1,64,64]{2,1,0:T(8,128)S(1)}, f32[1,64,64]{2,1,0:T(8,128)}, u32[]{:S(2)}) copy-start(f32[1,64,64]{2,1,0:T(8,128)} %param.12) | copy-start | bytes 49156
  0.0 22.4 %copy-start.12 = (s32[4]{0:T(128)S(1)}, s32[4]{0:T(128)}, u32[]{:S(2)}) copy-start(s32[4]{0:T(128)} %param.14) | copy-start | bytes 52
  0.0 23.0 %copy-start.13 = (s32[4]{0:T(128)S(1)}, s32[4]{0:T(128)}, u32[]{:S(2)}) copy-start(s32[4]{0:T(128)} %param.15) | copy-start | bytes 52
  0.0 23.1 %copy-start.6 = (f32[1,2]{1,0:T(1,128)S(1)}, f32[1,2]{1,0:T(1,128)}, u32[]{:S(2)}) copy-start(f32[1,2]{1,0:T(1,128)} %param.13) | copy-start | bytes 28
  0.0 23.6 %copy-start.1 = (bf16[1,2,64,16,128]{4,3,2,1,0:T(8,128)(2,1)S(1)}, bf16[1,2,64,16,128]{4,3,2,1,0:T(8,128)(2,1)}, u32[]{:S(2)}) copy-start(bf16[1,2,64,16,128]{4,3,2,1,0:T(8,128)(2,1)} %param.10) | copy-start | bytes 1572868
  0.0 25.0 %copy-start.11 = (f32[1,2,64]{2,1,0:T(2,128)S(1)}, f32[1,2,64]{2,1,0:T(2,128)}, u32[]{:S(2)}) copy-start(f32[1,2,64]{2,1,0:T(2,128)} %param.11) | copy-start | bytes 1540
  1.5 23.7 %collective-permute-start.4 = (f32[2,16,128]{2,1,0:T(8,128)S(1)}, f32[2,16,128]{2,1,0:T(8,128)S(1)}, u32[]{:S(2)}, u32[]{:S(2)}) collective-permute-start(f32[2,16,128]{2,1,0:T(8,128)S(1)} %fusion.8), channel_id=1, source_target_pairs={{0,384},{384,0},{1,385},{385,1},{2,386},{386,2},{3,387},{387,3},{4... | collective-permute-start | bytes 49160 | tf_op jit(solution)/shard_map/ppermute | solution.py:33
  3.5 23.1 %collective-permute-start = (f32[2,64,1,128]{3,2,0,1:T(1,128)S(1)}, f32[2,64,1,128]{3,2,0,1:T(1,128)S(1)}, u32[]{:S(2)}, u32[]{:S(2)}) collective-permute-start(f32[2,64,1,128]{3,2,0,1:T(1,128)S(1)} %get-tuple-element.15), channel_id=1, source_target_pairs={{4,0},{8,4},{12,8},{16,12},{20,16},{24,20},{28,24},{32,28},{36,32}... | collective-permute-start | bytes 196616 | tf_op jit(solution)/shard_map/ppermute | solution.py:19
  20.4 10.4 %collective-permute-start.1 = (f32[2,64,1,128]{3,2,0,1:T(1,128)S(1)}, f32[2,64,1,128]{3,2,0,1:T(1,128)S(1)}, u32[]{:S(2)}, u32[]{:S(2)}) collective-permute-start(f32[2,64,1,128]{3,2,0,1:T(1,128)S(1)} %get-tuple-element.14), channel_id=1, source_target_pairs={{0,4},{4,8},{8,12},{12,16},{16,20},{20,24},{24,28},{28,32},{32,36}... | collective-permute-start | bytes 196616 | tf_op jit(solution)/shard_map/ppermute | solution.py:17
  22.4 8.4 %copy-start.4 = (pred[4]{0:T(512)(128)(4,1)}, pred[4]{0:T(512)(128)(4,1)S(1)}, u32[]{:S(2)}) copy-start(pred[4]{0:T(512)(128)(4,1)S(1)} %get-tuple-element.6) | copy-start | bytes 16
  23.0 7.8 %copy-start.3 = (s32[1024]{0:T(1024)}, s32[1024]{0:T(1024)S(1)}, u32[]{:S(2)}) copy-start(s32[1024]{0:T(1024)S(1)} %pad_clamp_fusion.1) | copy-start | bytes 12292
  23.1 7.8 %copy-start.9 = (f32[4]{0:T(128)}, f32[4]{0:T(128)S(1)}, u32[]{:S(2)}) copy-start(f32[4]{0:T(128)S(1)} %subtract_convert_fusion) | copy-start | bytes 52
  23.1 7.7 %copy-start.2 = (s32[1024]{0:T(1024)}, s32[1024]{0:T(1024)S(1)}, u32[]{:S(2)}) copy-start(s32[1024]{0:T(1024)S(1)} %pad_clamp_fusion) | copy-start | bytes 12292
  34.7 6.8 %collective-permute-start.2 = (f32[2,64,18,1]{1,0,3,2:T(2,128)S(1)}, f32[2,64,18,1]{1,0,3,2:T(2,128)S(1)}, u32[]{:S(2)}, u32[]{:S(2)}) collective-permute-start(f32[2,64,18,1]{1,0,3,2:T(2,128)S(1)} %copy.91), channel_id=1, source_target_pairs={{1,0},{2,1},{3,2},{5,4},{6,5},{7,6},{9,8},{10,9},{11,10},{13,12},{... | collective-permute-start | bytes 27656 | tf_op jit(solution)/shard_map/ppermute | solution.py:19
  39.2 6.5 %collective-permute-start.3 = (f32[2,64,18,1]{1,0,3,2:T(2,128)S(1)}, f32[2,64,18,1]{1,0,3,2:T(2,128)S(1)}, u32[]{:S(2)}, u32[]{:S(2)}) collective-permute-start(f32[2,64,18,1]{1,0,3,2:T(2,128)S(1)} %copy.93), channel_id=1, source_target_pairs={{0,1},{1,2},{2,3},{4,5},{5,6},{6,7},{8,9},{9,10},{10,11},{12,13},{... | collective-permute-start | bytes 27656 | tf_op jit(solution)/shard_map/ppermute | solution.py:17
  41.4 6.2 %copy-start.7 = (f32[64]{0:T(128)S(1)}, f32[64]{0:T(128)}, u32[]{:S(2)}) copy-start(f32[64]{0:T(128)} %compare_convert_fusion) | copy-start | bytes 772
  52.4 9.5 %copy-start.5 = (pred[4]{0:T(512)(128)(4,1)S(1)}, pred[4]{0:T(512)(128)(4,1)}, u32[]{:S(2)}) copy-start(pred[4]{0:T(512)(128)(4,1)} %copy-done.4) | copy-start | bytes 16
  52.4 9.5 %copy-start.10 = (f32[4]{0:T(128)S(1)}, f32[4]{0:T(128)}, u32[]{:S(2)}) copy-start(f32[4]{0:T(128)} %copy-done.9) | copy-start | bytes 52
  53.1 7.9 %collective-permute-start.9 = (f32[2,16,128]{2,1,0:T(8,128)S(1)}, f32[2,16,128]{2,1,0:T(8,128)S(1)}, u32[]{:S(2)}, u32[]{:S(2)}) collective-permute-start(f32[2,16,128]{2,1,0:T(8,128)S(1)} %bitcast.51), channel_id=1, source_target_pairs={{0,384},{384,0},{1,385},{385,1},{2,386},{386,2},{3,387},{387,3},{4... | collective-permute-start | bytes 49160 | tf_op jit(solution)/shard_map/ppermute | solution.py:33
  55.1 7.6 %collective-permute-start.5 = (f32[2,64,1,128]{3,2,0,1:T(1,128)S(1)}, f32[2,64,1,128]{3,2,0,1:T(1,128)S(1)}, u32[]{:S(2)}, u32[]{:S(2)}) collective-permute-start(f32[2,64,1,128]{3,2,0,1:T(1,128)S(1)} %get-tuple-element.13), channel_id=1, source_target_pairs={{4,0},{8,4},{12,8},{16,12},{20,16},{24,20},{28,24},{32,28},{36,32}... | collective-permute-start | bytes 196616 | tf_op jit(solution)/shard_map/ppermute | solution.py:19
  59.1 10.4 %collective-permute-start.6 = (f32[2,64,1,128]{3,2,0,1:T(1,128)S(1)}, f32[2,64,1,128]{3,2,0,1:T(1,128)S(1)}, u32[]{:S(2)}, u32[]{:S(2)}) collective-permute-start(f32[2,64,1,128]{3,2,0,1:T(1,128)S(1)} %get-tuple-element.12), channel_id=1, source_target_pairs={{0,4},{4,8},{8,12},{12,16},{16,20},{20,24},{24,28},{28,32},{32,36}... | collective-permute-start | bytes 196616 | tf_op jit(solution)/shard_map/ppermute | solution.py:17
  73.3 7.3 %collective-permute-start.7 = (f32[2,64,18,1]{1,0,3,2:T(2,128)S(1)}, f32[2,64,18,1]{1,0,3,2:T(2,128)S(1)}, u32[]{:S(2)}, u32[]{:S(2)}) collective-permute-start(f32[2,64,18,1]{1,0,3,2:T(2,128)S(1)} %copy.107), channel_id=1, source_target_pairs={{1,0},{2,1},{3,2},{5,4},{6,5},{7,6},{9,8},{10,9},{11,10},{13,12},{... | collective-permute-start | bytes 27656 | tf_op jit(solution)/shard_map/ppermute | solution.py:19
  78.2 6.5 %collective-permute-start.8 = (f32[2,64,18,1]{1,0,3,2:T(2,128)S(1)}, f32[2,64,18,1]{1,0,3,2:T(2,128)S(1)}, u32[]{:S(2)}, u32[]{:S(2)}) collective-permute-start(f32[2,64,18,1]{1,0,3,2:T(2,128)S(1)} %copy.109), channel_id=1, source_target_pairs={{0,1},{1,2},{2,3},{4,5},{5,6},{6,7},{8,9},{9,10},{10,11},{12,13},{... | collective-permute-start | bytes 27656 | tf_op jit(solution)/shard_map/ppermute | solution.py:17
  80.6 6.0 %copy-start.8 = (f32[64]{0:T(128)S(1)}, f32[64]{0:T(128)}, u32[]{:S(2)}) copy-start(f32[64]{0:T(128)} %compare_convert_fusion) | copy-start | bytes 772
where the time goes:
time: 93.4 us; the launch traced here: 92.9 us
  starting transfers between devices  39.7 us (43%)
  local copies, waits for them, and re-layouts  20.4 us (22%)
  waiting for transfers between devices  18 us (19%)
  other arithmetic  10.9 us (12%)
  matrix products  3.41 us (4%)
    ppermute x4, starting transfers between devices, with_halo(): lax.ppermute(head, axis, [((i + 1) % count, i) for i in range(ends)])  29.2 us
    ppermute x4, waiting for transfers between devices, with_halo(): lax.ppermute(tail, axis, [(i, (i + 1) % count) for i in range(ends)])  18 us
    ppermute x4, starting transfers between devices, with_halo(): lax.ppermute(tail, axis, [(i, (i + 1) % count) for i in range(ends)])  6.59 us
    add x2, other arithmetic, advance(): updated = updated + level_pick[None, :, None, None] * increment[:, None]  6.13 us
    slice x6, local copies, waits for them, and re-layouts, with_halo(): lax.slice_in_dim(cells, cells.shape[dim] - width, cells.shape[dim], axis=...  4.64 us
    ppermute x2, starting transfers between devices, swapped(): return lax.ppermute(block, axis, route)  3.84 us
    slice x2, local copies, waits for them, and re-layouts, with_halo(): head = lax.slice_in_dim(cells, 0, width, axis=dim)  3.79 us
    ppermute x2, local copies, waits for them, and re-layouts, with_halo(): lax.ppermute(tail, axis, [(i, (i + 1) % count) for i in range(ends)])  3.64 us
  transfers between devices with their start and end apart: 10, of which 4 were waited for; matrix products, arithmetic and copies ran while one was open for 11% of the time, Pallas kernels for 0%

commit v1 on v0

v1 whole, which is shorter than its diff:
```python
import jax
import jax.numpy as jnp
from jax import lax
from jax.experimental import pallas as pl
from jax.experimental.pallas import tpu as pltpu
from jax.sharding import PartitionSpec as P

MESH = pl.DeviceIdType.MESH
F32 = jnp.float32
BF16 = jnp.bfloat16
EAST, WEST, NORTH, SOUTH, FLUID = range(5)


def split(value):
    high = value.astype(BF16)
    low = (value - high.astype(F32)).astype(BF16)
    return high, low


def stacked(value):
    high, low = split(value)
    return jnp.concatenate([high, high, low, low], axis=0)


def window_kernel(
    state, rows, flow, diffusion, solve, rate, block_map, ice_mask,
    out,
    q0, q1, res, flow_v, flow_n, half_c, half_d, kappa, diff_v, solve_v, lhs, surf_col,
    rate_s, map_s, ice_s,
    own_surf, other_surf, weights, increment,
    halo_e, halo_w, packed, pack_n, pack_s, flow_p, kappa_p, placed,
    load_sem, small_sem, send_sem, recv_sem, out_sem,
):
    fluid = lax.axis_index("fluid")
    zon = lax.axis_index("zon")
    mer = lax.axis_index("mer")
    zons = lax.axis_size("zon")
    mers = lax.axis_size("mer")
    levels, columns = 64, 16
    peers = (
        (fluid, lax.rem(zon + 1, zons), mer),
        (fluid, lax.rem(zon + zons - 1, zons), mer),
        (fluid, zon, lax.rem(mer + 1, mers)),
        (fluid, zon, lax.rem(mer + mers - 1, mers)),
        (1 - fluid, zon, mer),
    )
    barrier = pltpu.get_barrier_semaphore()
    for peer in peers:
        pl.semaphore_signal(barrier, inc=1, device_id=peer, device_id_type=MESH)

    surface = (levels - 1) * (1 - fluid)
    is_atm = fluid == 0

    smalls = [
        pltpu.make_async_copy(block_map, map_s, small_sem.at[0]),
        pltpu.make_async_copy(ice_mask, ice_s, small_sem.at[1]),
        pltpu.make_async_copy(rate, rate_s, small_sem.at[2]),
        pltpu.make_async_copy(solve, solve_v, small_sem.at[3]),
        pltpu.make_async_copy(diffusion, diff_v, small_sem.at[4]),
        pltpu.make_async_copy(state.at[:, surface], own_surf.at[0], small_sem.at[5]),
    ]
    flow_load = pltpu.make_async_copy(flow, flow_v, load_sem.at[columns])
    flow_load.start()
    loads = []
    for x in range(columns):
        load = pltpu.make_async_copy(rows.at[:, :, x, 0, :], q0.at[x + 1], load_sem.at[x])
        load.start()
        loads.append(load)
    for copy in smalls:
        copy.start()

    pl.semaphore_wait(barrier, 5)

    def send(step, way, source, target):
        slot = step * 5 + way
        copy = pltpu.make_async_remote_copy(
            src_ref=source,
            dst_ref=target,
            send_sem=send_sem.at[slot],
            recv_sem=recv_sem.at[slot],
            device_id=peers[way],
            device_id_type=MESH,
        )
        copy.start()
        return copy

    sends = [{}, {}]
    sends[0][EAST] = send(0, EAST, rows.at[:, :, columns - 1, 0, :], halo_w.at[0])
    sends[0][WEST] = send(0, WEST, rows.at[:, :, 0, 0, :], halo_e.at[0])
    sends[0][FLUID] = send(0, FLUID, state.at[:, surface], other_surf.at[0])

    lane = lax.broadcasted_iota(jnp.int32, (levels, 128), 1)
    lane32 = lax.broadcasted_iota(jnp.int32, (32, 128), 1)
    zero_block = jnp.zeros((2, levels, 128), F32)
    for field in (q0, q1):
        field[0] = zero_block
        field[columns + 1] = zero_block
    for load in loads:
        load.wait()

    def packed_lanes(block, j, total):
        for half in range(2):
            start = 64 * half + 2 * j
            part = block[32 * half : 32 * half + 32]
            total = jnp.where((lane32 >> 1) == (start >> 1), pltpu.roll(part, (start + 1) % 128, 1), total)
        return total

    def pack(field, offset):
        total = jnp.zeros((32, 128), F32)
        for x in range(columns):
            for t in range(2):
                total = packed_lanes(field[x + offset, t], 2 * x + t, total)
        return total

    packed[0] = pack(q0, 1)
    sends[0][NORTH] = send(0, NORTH, packed.at[0], pack_s.at[0])
    sends[0][SOUTH] = send(0, SOUTH, packed.at[0], pack_n.at[0])

    for copy in smalls:
        copy.wait()
    eye = lax.broadcasted_iota(jnp.int32, (levels, levels), 0) == lax.broadcasted_iota(jnp.int32, (levels, levels), 1)
    for t in range(2):
        line = jnp.broadcast_to(diff_v[t : t + 1, :], (levels, levels))
        kappa[t] = jnp.broadcast_to(jnp.sum(jnp.where(eye, line, 0.0), axis=1, keepdims=True), (levels, 128))
    matrix = solve_v[...]
    twice = jnp.concatenate([matrix, matrix], axis=1)
    high = twice.astype(BF16).astype(F32)
    pair = jnp.where(lane < levels, high, twice - high)
    lhs[...] = jnp.concatenate([pair, pair], axis=1).astype(BF16)
    at_surface = lax.broadcasted_iota(jnp.int32, (levels, levels), 1) == surface
    surf_col[...] = jnp.broadcast_to(
        jnp.sum(jnp.where(at_surface, matrix, 0.0), axis=1, keepdims=True), (levels, 128)
    )
    block_of = lax.broadcasted_iota(jnp.int32, (8, 128), 1) // 32
    for k in range(4):
        line = jnp.zeros((8, 128), F32)
        for o in range(4):
            b = (o + k) % 4
            base = 4 * mer
            ocean_hit = jnp.where(map_s[o] - base == b, 1 - ice_s[o], 0)
            atm_hit = jnp.where(map_s[b] - base == o, 1 - ice_s[b], 0)
            hit = jnp.where(is_atm, atm_hit, ocean_hit).astype(F32)
            line = jnp.where(block_of == o, hit, line)
        weights[k] = line

    flow_load.wait()
    for part, half in ((0, half_c), (1, half_d)):
        flow_n[part] = flow_v[part].astype(F32).reshape(levels * columns, 128) * 0.5
        for x in range(columns):
            half[x] = flow_n[part, pl.ds(x, levels, stride=columns), :]
    total = jnp.zeros((32, 128), F32)
    for x in range(columns):
        block = half_d[x]
        for t in range(2):
            total = packed_lanes(block, 2 * x + t, total)
    flow_p[...] = total
    quarter = (lane32 >> 1) & 1
    kappa_p[...] = jnp.where(
        quarter == 0,
        jnp.where(lane32 < 64, kappa[0, 0:32], kappa[0, 32:64]),
        jnp.where(lane32 < 64, kappa[1, 0:32], kappa[1, 32:64]),
    )

    def solve_of(value):
        return jnp.dot(lhs[...], stacked(value), preferred_element_type=F32)

    def interior(field, target, offset):
        def body(x, carry):
            parts = []
            c = half_c[x]
            d = half_d[x]
            for t in range(2):
                k = kappa[t]
                q = field[x + 1, t]
                north = jnp.where(lane == 127, 0.0, pltpu.roll(q, 127, 1))
                south = jnp.where(lane == 0, 0.0, pltpu.roll(q, 1, 1))
                parts.append(
                    (1.0 - 4.0 * k) * q
                    + (k - c) * field[x + 2, t]
                    + (k + c) * field[x, t]
                    + (k - d) * north
                    + (k + d) * south
                )
            solved = solve_of(jnp.concatenate(parts, axis=1))
            target[x + offset, 0] = solved[:, :128]
            target[x + offset, 1] = solved[:, 128:]
            return carry

        lax.fori_loop(0, columns, body, 0, unroll=2)

    def corrections(step, target, offset, first, each):
        sends[step][EAST].wait_recv()
        sends[step][WEST].wait_recv()
        ends = []
        for t in range(2):
            ends.append((kappa[t] + half_c[0]) * halo_w[step, t])
        for t in range(2):
            ends.append((kappa[t] - half_c[columns - 1]) * halo_e[step, t])
        solved_ends = solve_of(jnp.concatenate(ends, axis=1))
        sends[step][FLUID].wait_recv()
        openness = weights[0] + weights[1] + weights[2] + weights[3]
        openness = jnp.concatenate([openness, openness], axis=0)
        for t in range(2):
            other = other_surf[step, t]
            flux = -openness * own_surf[step, t]
            for k in range(4):
                rolled = other if k == 0 else pltpu.roll(other, 128 - 32 * k, 1)
                flux = flux + jnp.concatenate([weights[k], weights[k]], axis=0) * rolled
            increment[step, t] = flux * rate_s[0, t]
        sends[step][NORTH].wait_recv()
        sends[step][SOUTH].wait_recv()
        has_north = jnp.where(mer == mers - 1, 0.0, 1.0)
        has_south = jnp.where(mer == 0, 0.0, 1.0)
        even = (lane32 & 1) == 0
        near = jnp.where(
            even,
            pltpu.roll(pack_n[step], 127, 1) * has_north,
            pltpu.roll(pack_s[step], 1, 1) * has_south,
        )
        terms = (kappa_p[...] + jnp.where(even, -flow_p[...], flow_p[...])) * near
        sides = solve_of(jnp.concatenate([terms, pltpu.roll(terms, 64, 1)], axis=0))
        edge = (lane == 0) | (lane == 127)
        column = surf_col[...]

        def correct(x, extra):
            for t in range(2):
                j = 2 * x + t
                value = target[x + offset, t] + column * increment[step, t, x : x + 1, :]
                value = value + jnp.where(edge, pltpu.roll(sides, (127 - 2 * j) % 128, 1), 0.0)
                if extra is not None:
                    value = value + extra[t]
                target[x + offset, t] = value
            each(x)

        correct(0, (solved_ends[:, 0:128], solved_ends[:, 128:256]))
        correct(columns - 1, (solved_ends[:, 256:384], solved_ends[:, 384:512]))
        first()
        for x in range(1, columns - 1):
            correct(x, None)

    interior(q0, q1, 1)

    def send_ends():
        sends[1][EAST] = send(1, EAST, q1.at[columns], halo_w.at[1])
        sends[1][WEST] = send(1, WEST, q1.at[1], halo_e.at[1])

    def keep_surface(x):
        for t in range(2):
            own_surf[1, t, x : x + 1, :] = q1[x + 1, t, pl.ds(surface, 1), :]

    corrections(0, q1, 1, send_ends, keep_surface)
    sends[1][FLUID] = send(1, FLUID, own_surf.at[1], other_surf.at[1])
    packed[1] = pack(q1, 1)
    sends[1][NORTH] = send(1, NORTH, packed.at[1], pack_s.at[1])
    sends[1][SOUTH] = send(1, SOUTH, packed.at[1], pack_n.at[1])

    interior(q1, res, 0)
    stores = []

    def store(x):
        copy = pltpu.make_async_copy(res.at[x], out.at[:, :, x, 0, :], out_sem.at[x])
        copy.start()
        stores.append(copy)

    corrections(1, res, 0, lambda: None, store)
    for copy in stores:
        copy.wait()
    for step in range(2):
        for way in range(5):
            sends[step][way].wait_send()


def on_device(state, flow, diffusion, column_solve, exchange_rate, block_map, ice_mask):
    _, tracers, levels, columns, merid = state.shape
    local = state.reshape(tracers, levels, columns, merid)
    rows = state.reshape(tracers, levels, columns, 1, merid)
    vmem = pltpu.VMEM
    dma = pltpu.SemaphoreType.DMA
    hbm = pl.BlockSpec(memory_space=pltpu.MemorySpace.HBM)
    result = pl.pallas_call(
        window_kernel,
        out_shape=jax.ShapeDtypeStruct((tracers, levels, columns, 1, merid), F32),
        in_specs=[hbm] * 8,
        out_specs=hbm,
        scratch_shapes=[
            vmem((columns + 2, tracers, levels, merid), F32),
            vmem((columns + 2, tracers, levels, merid), F32),
            vmem((columns, tracers, levels, merid), F32),
            vmem((2, levels, columns, merid), BF16),
            vmem((2, levels * columns, merid), F32),
            vmem((columns, levels, merid), F32),
            vmem((columns, levels, merid), F32),
            vmem((tracers, levels, merid), F32),
            vmem((tracers, levels), F32),
            vmem((levels, levels), F32),
            vmem((levels, 4 * levels), BF16),
            vmem((levels, merid), F32),
            pltpu.SMEM((1, tracers), F32),
            pltpu.SMEM((4,), jnp.int32),
            pltpu.SMEM((4,), jnp.int32),
            vmem((2, tracers, columns, merid), F32),
            vmem((2, tracers, columns, merid), F32),
            vmem((4, 8, merid), F32),
            vmem((2, tracers, columns, merid), F32),
            vmem((2, tracers, levels, merid), F32),
            vmem((2, tracers, levels, merid), F32),
            vmem((2, 32, merid), F32),
            vmem((2, 32, merid), F32),
            vmem((2, 32, merid), F32),
            vmem((32, merid), F32),
            vmem((32, merid), F32),
            vmem((32, merid), F32),
            dma((columns + 1,)),
            dma((6,)),
            dma((10,)),
            dma((10,)),
            dma((columns,)),
        ],
        compiler_params=pltpu.CompilerParams(
            collective_id=0, has_side_effects=True, vmem_limit_bytes=60 * 2**20
        ),
    )(
        local,
        rows,
        flow.reshape(2, levels, columns, merid),
        diffusion.reshape(tracers, levels),
        column_solve.reshape(levels, levels),
        exchange_rate,
        block_map,
        ice_mask,
    )
    return result.reshape(1, tracers, levels, columns, merid)


def solution(mesh):
    return jax.shard_map(
        on_device,
        mesh=mesh,
        in_specs=(
            P("fluid", None, None, "zon", "mer"),
            P("fluid", None, None, "zon", "mer"),
            P("fluid", None, None),
            P("fluid", None, None),
            P("fluid", None),
            P("mer"),
            P("mer"),
        ),
        out_specs=P("fluid", None, None, "zon", "mer"),
        check_vma=False,
    )
```

time: 93.4 us -> 33.3 us (0.36)
  the two profiles are of different devices: /device:TPU:48 before, /device:TPU:1 now
where the time goes in v1:
time: 33.3 us; the launch traced here: 33.1 us
  Pallas kernels  30.8 us (92%)
  local copies, waits for them, and re-layouts  2.26 us (7%)
    pallas_call x1, Pallas kernels, on_device(): pl.pallas_call(window_kernel, out_shape=jax.ShapeDtypeStruct((tracers, le...  30.8 us
    unnamed x1, local copies, waits for them, and re-layouts  2.26 us

profile of v1, /device:TPU:1, one launch (start us, length us, event | category | flops | bytes accessed | tf_op | source)
XLA Modules:
  0.0 33.1 jit_solution(5911141384959116776)
XLA Ops:
  0.0 30.8 %shard_map.73 = f32[2,64,16,1,128]{4,3,2,1,0:T(1,128)} custom-call(f32[2,64,16,128]{3,2,1,0:T(8,128)} %bitcast.6, f32[2,64,16,1,128]{4,3,2,1,0:T(1,128)} %bitcast.7, bf16[2,64,16,128]{3,2,1,0:T(8,128)(2,1)} %bitcast.9, f32[2,64]{1,0:T(2,128)} %bitcast.11, f32[64,64]{1,0:T(8,128)} %bitcast.10, f32[1,2]{1,0:T(1,128)} %rate.1, s32[4]{0:T(128)} %block_map.1, ...), custom_call_target="tpu_custom_call" | custom-call | tf_op jit(solution)/shard_map/pallas_call | solution.py:280
  30.8 2.3 %copy.9 = f32[1,2,64,16,128]{4,3,2,1,0:T(8,128)} copy(f32[1,2,64,16,128]{4,3,2,1,0:T(8,128)} %bitcast.8) | data formatting | bytes 2097152

commit v2 on v1

v2 whole, which is shorter than its diff:
```python
import jax
import jax.numpy as jnp
from jax import lax
from jax.experimental import pallas as pl
from jax.experimental.pallas import tpu as pltpu
from jax.sharding import PartitionSpec as P

MESH = pl.DeviceIdType.MESH
F32 = jnp.float32
BF16 = jnp.bfloat16


def split(value):
    high = value.astype(BF16)
    low = (value - high.astype(F32)).astype(BF16)
    return high, low


def stacked(value):
    high, low = split(value)
    return jnp.concatenate([high, high, low, low], axis=0)


def window_kernel(
    state, rows, flow, diffusion, solve, rate, block_map, ice_mask,
    res,
    q0, q1, flow_v, flow_n, half_c, half_d, kappa, diff_v, solve_v, lhs, surf_col,
    rate_s, map_s, ice_s,
    own_surf, other_surf, own_late, other_late, west_surf, weights, increment,
    halo_e, west_out, west_in, west_row, ring_out, ring_in,
    mini_out, mini_in, corner_out, corner_n, corner_s,
    pack_out, pack_n, pack_s, pack2_out, pack2_n, pack2_s, flow_p, kappa_p,
    load_sem, small_sem, send_sem, recv_sem,
):
    fluid = lax.axis_index("fluid")
    zon = lax.axis_index("zon")
    mer = lax.axis_index("mer")
    zons = lax.axis_size("zon")
    mers = lax.axis_size("mer")
    levels, columns = 64, 16
    last = columns - 1
    east, west = lax.rem(zon + 1, zons), lax.rem(zon + zons - 1, zons)
    north, south = lax.rem(mer + 1, mers), lax.rem(mer + mers - 1, mers)
    across = 1 - fluid
    barrier = pltpu.get_barrier_semaphore()
    for peer in (
        (fluid, west, mer),
        (fluid, west, north),
        (fluid, west, south),
        (across, west, mer),
        (fluid, zon, north),
        (fluid, zon, south),
        (across, zon, mer),
    ):
        pl.semaphore_signal(barrier, inc=1, device_id=peer, device_id_type=MESH)

    surface = (levels - 1) * (1 - fluid)
    is_atm = fluid == 0

    flow_load = pltpu.make_async_copy(flow, flow_v, load_sem.at[columns])
    flow_load.start()
    loads = []
    for x in range(columns):
        load = pltpu.make_async_copy(rows.at[:, :, x, 0, :], q0.at[x + 1], load_sem.at[x])
        load.start()
        loads.append(load)
    smalls = [
        pltpu.make_async_copy(block_map, map_s, small_sem.at[0]),
        pltpu.make_async_copy(ice_mask, ice_s, small_sem.at[1]),
        pltpu.make_async_copy(rate, rate_s, small_sem.at[2]),
        pltpu.make_async_copy(solve, solve_v, small_sem.at[3]),
        pltpu.make_async_copy(diffusion, diff_v, small_sem.at[4]),
        pltpu.make_async_copy(state.at[:, surface], own_surf.at[0], small_sem.at[5]),
    ]
    for copy in smalls:
        copy.start()

    sent = []

    def copy_to(slot, peer, source, target):
        return pltpu.make_async_remote_copy(
            src_ref=source,
            dst_ref=target,
            send_sem=send_sem.at[slot],
            recv_sem=recv_sem.at[slot],
            device_id=peer,
            device_id_type=MESH,
        )

    row_w = copy_to(0, (fluid, east, mer), west_out, west_in)
    surf_w = copy_to(1, (across, east, mer), rows.at[:, surface, last, 0, :], west_surf)
    surf_0 = copy_to(2, (across, zon, mer), state.at[:, surface], other_surf.at[0])
    corner_to_n = copy_to(3, (fluid, east, north), corner_out, corner_s)
    corner_to_s = copy_to(4, (fluid, east, south), corner_out, corner_n)
    ring = copy_to(5, (fluid, east, mer), ring_out, ring_in)
    mini_w = copy_to(6, (fluid, east, mer), mini_out, mini_in)
    pack_to_n = copy_to(7, (fluid, zon, north), pack_out, pack_s)
    pack_to_s = copy_to(8, (fluid, zon, south), pack_out, pack_n)
    row_e = copy_to(9, (fluid, west, mer), rows.at[:, :, 0, 0, :], halo_e.at[0])
    surf_1 = copy_to(10, (across, zon, mer), own_surf.at[1], other_surf.at[1])
    pack2_to_n = copy_to(11, (fluid, zon, north), pack2_out, pack2_s)
    pack2_to_s = copy_to(12, (fluid, zon, south), pack2_out, pack2_n)
    surf_late = copy_to(13, (across, zon, mer), own_late, other_late)
    row2_e = copy_to(14, (fluid, west, mer), q1.at[1], halo_e.at[1])

    def send(*copies):
        for copy in copies:
            copy.start()
            sent.append(copy)

    lane = lax.broadcasted_iota(jnp.int32, (levels, 128), 1)
    lane32 = lax.broadcasted_iota(jnp.int32, (32, 128), 1)
    even = (lane32 & 1) == 0
    edge = (lane == 0) | (lane == 127)

    def packed_lanes(block, j, total):
        for half in range(2):
            start = 64 * half + 2 * j
            piece = block[32 * half : 32 * half + 32]
            total = jnp.where((lane32 >> 1) == (start >> 1), pltpu.roll(piece, (start + 1) % 128, 1), total)
        return total

    def pack(field):
        total = jnp.zeros((32, 128), F32)
        for x in range(columns):
            for t in range(2):
                total = packed_lanes(field[x + 1, t], 2 * x + t, total)
        return total

    lane8 = lax.broadcasted_iota(jnp.int32, (8, 128), 1)

    def mini(total):
        small = jnp.zeros((8, 128), F32)
        for i in range(4):
            piece = total[8 * i : 8 * i + 8]
            small = jnp.where(((lane8 >> 2) & 15) == 15 - i, pltpu.roll(piece, (128 - 4 * i) % 128, 1), small)
        return small

    def from_mini(small):
        return jnp.concatenate([small] + [pltpu.roll(small, 4 * i, 1) for i in range(1, 4)], axis=0)

    def unpacked(terms):
        return jnp.concatenate([terms, pltpu.roll(terms, 64, 1)], axis=0)

    def at_edges(sides, j):
        return pltpu.roll(sides, (127 - 2 * j) % 128, 1)

    for copy in smalls:
        copy.wait()
    eye = lax.broadcasted_iota(jnp.int32, (levels, levels), 0) == lax.broadcasted_iota(jnp.int32, (levels, levels), 1)
    for t in range(2):
        line = jnp.broadcast_to(diff_v[t : t + 1, :], (levels, levels))
        kappa[t] = jnp.broadcast_to(jnp.sum(jnp.where(eye, line, 0.0), axis=1, keepdims=True), (levels, 128))
    matrix = solve_v[...]
    twice = jnp.concatenate([matrix, matrix], axis=1)
    high = twice.astype(BF16).astype(F32)
    pair = jnp.where(lane < levels, high, twice - high)
    lhs[...] = jnp.concatenate([pair, pair], axis=1).astype(BF16)
    at_surface = lax.broadcasted_iota(jnp.int32, (levels, levels), 1) == surface
    surf_col[...] = jnp.broadcast_to(
        jnp.sum(jnp.where(at_surface, matrix, 0.0), axis=1, keepdims=True), (levels, 128)
    )
    quarter = (lane32 >> 1) & 1
    kappa_p[...] = jnp.where(
        quarter == 0,
        jnp.where(lane32 < 64, kappa[0, 0:32], kappa[0, 32:64]),
        jnp.where(lane32 < 64, kappa[1, 0:32], kappa[1, 32:64]),
    )
    zero_block = jnp.zeros((2, levels, 128), F32)
    for field in (q0, q1):
        field[0] = zero_block
        field[columns + 1] = zero_block

    flow_load.wait()
    for piece, half in ((0, half_c), (1, half_d)):
        flow_n[piece] = flow_v[piece].astype(F32).reshape(levels * columns, 128) * 0.5
        for x in range(columns):
            half[x] = flow_n[piece, pl.ds(x, levels, stride=columns), :]
    total = jnp.zeros((32, 128), F32)
    for x in range(columns):
        block = half_d[x]
        for t in range(2):
            total = packed_lanes(block, 2 * x + t, total)
    flow_p[...] = total
    mini_out[...] = mini(total)
    ring_out[0] = half_c[last].astype(BF16)
    for load in loads:
        load.wait()

    def solve_of(value):
        return jnp.dot(lhs[...], stacked(value), preferred_element_type=F32)

    def interior(field, target, offset, x):
        c = half_c[x]
        d = half_d[x]
        parts = []
        for t in range(2):
            k = kappa[t]
            q = field[x + 1, t]
            parts.append(
                (1.0 - 4.0 * k) * q
                + (k - c) * field[x + 2, t]
                + (k + c) * field[x, t]
                + (k - d) * jnp.where(lane == 127, 0.0, pltpu.roll(q, 127, 1))
                + (k + d) * jnp.where(lane == 0, 0.0, pltpu.roll(q, 1, 1))
            )
        solved = solve_of(jnp.concatenate(parts, axis=1))
        target[x + offset, 0] = solved[:, :128]
        target[x + offset, 1] = solved[:, 128:]

    interior(q0, q1, 1, last)
    ring_out[1:3] = q1[columns].astype(BF16)
    west_out[...] = q0[columns].astype(BF16)
    total = pack(q0)
    pack_out[0:32] = total
    corner_out[...] = mini(total)
    ends = jnp.zeros((32, 128), F32)
    for t in range(2):
        ends = packed_lanes(half_c[0], 2 * last + t, ends)
    pack_out[32:40] = mini(ends)

    pl.semaphore_wait(barrier, 7)
    send(row_w, ring, mini_w, corner_to_n, corner_to_s, surf_w, surf_0, pack_to_n, pack_to_s)

    block_of = lax.broadcasted_iota(jnp.int32, (8, 128), 1) // 32
    base = 4 * mer
    for k in range(4):
        line = jnp.zeros((8, 128), F32)
        for o in range(4):
            b = (o + k) % 4
            ocean_hit = jnp.where(map_s[o] - base == b, 1 - ice_s[o], 0)
            atm_hit = jnp.where(map_s[b] - base == o, 1 - ice_s[b], 0)
            hit = jnp.where(is_atm, atm_hit, ocean_hit).astype(F32)
            line = jnp.where(block_of == o, hit, line)
        weights[k] = line

    def first_body(x, carry):
        interior(q0, q1, 1, x)
        return carry

    lax.fori_loop(0, last, first_body, 0, unroll=3)

    def exchange(own, other, repeat):
        shares = [jnp.concatenate([weights[k]] * repeat, axis=0) if repeat else weights[k][0:2] for k in range(4)]
        flux = -(shares[0] + shares[1] + shares[2] + shares[3]) * own
        for k in range(4):
            flux = flux + shares[k] * (other if k == 0 else pltpu.roll(other, 128 - 32 * k, 1))
        return flux

    def increments(step):
        for t in range(2):
            increment[step, t] = exchange(own_surf[step, t], other_surf[step, t], 2) * rate_s[0, t]

    has_north = jnp.where(mer == mers - 1, 0.0, 1.0)
    has_south = jnp.where(mer == 0, 0.0, 1.0)

    def near(from_n, from_s):
        return jnp.where(even, pltpu.roll(from_n, 127, 1) * has_north, pltpu.roll(from_s, 1, 1) * has_south)

    def side_terms(beyond, half):
        return (kappa_p[...] + jnp.where(even, -half, half)) * beyond

    def greet_west():
        row_w.wait_recv()
        row_e.start()

    sent.append(row_e)
    seam = lax.rem(zon, 24) == 0
    pl.when(jnp.logical_not(seam))(greet_west)

    surf_0.wait_recv()
    increments(0)
    pack_to_n.wait_recv()
    pack_to_s.wait_recv()
    sides = solve_of(unpacked(side_terms(near(pack_n[0:32], pack_s[0:32]), flow_p[...])))
    column = surf_col[...]

    def corrected(step, target, offset, x):
        return [
            target[x + offset, t]
            + column * increment[step, t, x : x + 1, :]
            + jnp.where(edge, at_edges(sides, 2 * x + t), 0.0)
            for t in range(2)
        ]

    def keep(x, values):
        for t in range(2):
            q1[x + 1, t] = values[t]
            own_surf[1, t, x : x + 1, :] = q1[x + 1, t, pl.ds(surface, 1), :]

    for x in range(last):
        keep(x, corrected(0, q1, 1, x))
    row_e.wait_recv()
    k_c = [kappa[t] - half_c[last] for t in range(2)]
    solved = solve_of(jnp.concatenate([k_c[t] * halo_e[0, t] for t in range(2)], axis=1))
    values = corrected(0, q1, 1, last)
    keep(last, [values[0] + solved[:, :128], values[1] + solved[:, 128:]])
    send(surf_1)
    pack2_out[...] = pack(q1)
    send(pack2_to_n, pack2_to_s)

    def second_body(x, carry):
        interior(q1, res, 0, x)
        return carry

    lax.fori_loop(2, columns, second_body, 0, unroll=2)
    surf_1.wait_recv()
    increments(1)
    pack2_to_n.wait_recv()
    pack2_to_s.wait_recv()
    beyond = near(pack2_n[...], pack2_s[...])
    sides = solve_of(unpacked(side_terms(beyond, flow_p[...])))
    for x in range(2, columns):
        values = corrected(1, res, 0, x)
        for t in range(2):
            res[x, t] = values[t]
    beyond = unpacked(beyond)

    pl.when(seam)(greet_west)
    ring.wait_recv()
    mini_w.wait_recv()
    corner_to_n.wait_recv()
    corner_to_s.wait_recv()
    west_row[...] = west_in[...].astype(F32)
    k_c = [kappa[t] + half_c[0] for t in range(2)]
    k_w = [kappa[t] - ring_in[0].astype(F32) for t in range(2)]
    from_n = from_mini(corner_n[...])
    from_s = from_mini(corner_s[...])
    corners = side_terms(near(from_n, from_s), from_mini(mini_in[...]))
    mixed = jnp.where(
        even,
        (kappa_p[...] + from_mini(pack_s[32:40])) * from_s * has_south,
        (kappa_p[...] + from_mini(pack_n[32:40])) * from_n * has_north,
    )
    solved = solve_of(
        jnp.concatenate(
            [k_c[t] * west_row[t] for t in range(2)]
            + [k_w[t] * q0[1, t] for t in range(2)]
            + [unpacked(corners), unpacked(mixed)],
            axis=1,
        )
    )
    pieces = [solved[:, 128 * i : 128 * i + 128] for i in range(6)]
    firsts = [q1[1, t] + pieces[t] for t in range(2)]
    for t in range(2):
        q1[1, t] = firsts[t]
        own_late[t : t + 1, :] = q1[1, t, pl.ds(surface, 1), :]
    send(surf_late, row2_e)
    shift = jnp.where((lane & 1) == 0, pltpu.roll(pieces[5], 67, 1), pltpu.roll(pieces[5], 69, 1))
    beyond_first = beyond + shift
    tracer = lax.broadcasted_iota(jnp.int32, (2, 128), 0)
    rates = jnp.where(tracer == 0, rate_s[0, 0], rate_s[0, 1])
    surf_w.wait_recv()
    west_own = jnp.concatenate([west_row[t, pl.ds(surface, 1), :] for t in range(2)], axis=0)
    west_flux = exchange(west_own, west_surf[...], 0) * rates
    wests = [
        ring_in[1 + t].astype(F32)
        + pieces[2 + t]
        + column * west_flux[t : t + 1]
        + jnp.where(edge, at_edges(pieces[4], 2 * last + t), 0.0)
        for t in range(2)
    ]

    def full(k, c, d, q, to_east, to_west, around):
        return (
            (1.0 - 4.0 * k) * q
            + (k - c) * to_east
            + (k + c) * to_west
            + (k - d) * jnp.where(lane == 127, around, pltpu.roll(q, 127, 1))
            + (k + d) * jnp.where(lane == 0, around, pltpu.roll(q, 1, 1))
        )

    updates = [
        full(kappa[t], half_c[0], half_d[0], firsts[t], q1[2, t], wests[t], at_edges(beyond_first, t)) for t in range(2)
    ] + [
        full(kappa[t], half_c[1], half_d[1], q1[2, t], q1[3, t], firsts[t], at_edges(beyond, 2 + t)) for t in range(2)
    ]
    solved = solve_of(jnp.concatenate(updates, axis=1))
    for t in range(2):
        res[1, t] = solved[:, 256 + 128 * t : 384 + 128 * t] + column * increment[1, t, 1:2, :]
    surf_late.wait_recv()
    late_flux = exchange(own_late[...], other_late[...], 0) * rates
    for t in range(2):
        res[0, t] = solved[:, 128 * t : 128 * t + 128] + column * late_flux[t : t + 1]

    row2_e.wait_recv()
    solved = solve_of(
        jnp.concatenate([(kappa[t] - half_c[last]) * halo_e[1, t] for t in range(2)], axis=1)
    )
    for t in range(2):
        res[last, t] = res[last, t] + solved[:, 128 * t : 128 * t + 128]
    for copy in sent:
        copy.wait_send()


def finish_kernel(source, out, sem):
    copies = [pltpu.make_async_copy(source.at[x], out.at[:, :, x, 0, :], sem.at[x]) for x in range(16)]
    for copy in copies:
        copy.start()
    for copy in copies:
        copy.wait()


def on_device(state, flow, diffusion, column_solve, exchange_rate, block_map, ice_mask):
    _, tracers, levels, columns, merid = state.shape
    local = state.reshape(tracers, levels, columns, merid)
    rows = state.reshape(tracers, levels, columns, 1, merid)
    vmem = pltpu.VMEM
    dma = pltpu.SemaphoreType.DMA
    hbm = pl.BlockSpec(memory_space=pltpu.MemorySpace.HBM)
    result = pl.pallas_call(
        window_kernel,
        out_shape=jax.ShapeDtypeStruct((columns, tracers, levels, merid), F32),
        in_specs=[hbm] * 8,
        out_specs=pl.BlockSpec(memory_space=pltpu.VMEM),
        scratch_shapes=[
            vmem((columns + 2, tracers, levels, merid), F32),
            vmem((columns + 2, tracers, levels, merid), F32),
            vmem((2, levels, columns, merid), BF16),
            vmem((2, levels * columns, merid), F32),
            vmem((columns, levels, merid), F32),
            vmem((columns, levels, merid), F32),
            vmem((tracers, levels, merid), F32),
            vmem((tracers, levels), F32),
            vmem((levels, levels), F32),
            vmem((levels, 4 * levels), BF16),
            vmem((levels, merid), F32),
            pltpu.SMEM((1, tracers), F32),
            pltpu.SMEM((4,), jnp.int32),
            pltpu.SMEM((4,), jnp.int32),
            vmem((2, tracers, columns, merid), F32),
            vmem((2, tracers, columns, merid), F32),
            vmem((tracers, merid), F32),
            vmem((tracers, merid), F32),
            vmem((tracers, merid), F32),
            vmem((4, 8, merid), F32),
            vmem((2, tracers, columns, merid), F32),
            vmem((2, tracers, levels, merid), F32),
            vmem((tracers, levels, merid), BF16),
            vmem((tracers, levels, merid), BF16),
            vmem((tracers, levels, merid), F32),
            vmem((tracers + 1, levels, merid), BF16),
            vmem((tracers + 1, levels, merid), BF16),
        ]
        + [vmem((8, merid), F32)] * 5
        + [vmem((40, merid), F32)] * 3
        + [vmem((32, merid), F32)] * 5
        + [
            dma((columns + 1,)),
            dma((6,)),
            dma((15,)),
            dma((15,)),
        ],
        compiler_params=pltpu.CompilerParams(
            collective_id=0, has_side_effects=True, vmem_limit_bytes=48 * 2**20
        ),
    )(
        *(pltpu.with_memory_space_constraint(v, pltpu.MemorySpace.HBM) for v in (
        local,
        rows,
        flow.reshape(2, levels, columns, merid),
        diffusion.reshape(tracers, levels),
        column_solve.reshape(levels, levels),
        exchange_rate,
        block_map,
        ice_mask,
    )))
    result = pl.pallas_call(
        finish_kernel,
        out_shape=jax.ShapeDtypeStruct((tracers, levels, columns, 1, merid), F32),
        in_specs=[pl.BlockSpec(memory_space=pltpu.VMEM)],
        out_specs=hbm,
        scratch_shapes=[dma((16,))],
        compiler_params=pltpu.CompilerParams(vmem_limit_bytes=48 * 2**20),
    )(result)
    return result.reshape(1, tracers, levels, columns, merid)


def solution(mesh):
    return jax.shard_map(
        on_device,
        mesh=mesh,
        in_specs=(
            P("fluid", None, None, "zon", "mer"),
            P("fluid", None, None, "zon", "mer"),
            P("fluid", None, None),
            P("fluid", None, None),
            P("fluid", None),
            P("mer"),
            P("mer"),
        ),
        out_specs=P("fluid", None, None, "zon", "mer"),
        check_vma=False,
    )
```

time: 33.3 us -> 30.1 us (0.904)
  the two profiles are of different devices: /device:TPU:1 before, /device:TPU:710 now
where the time goes in v2:
time: 30.1 us; the launch traced here: 29.9 us
  Pallas kernels  29.9 us (99%)
    pallas_call x1, Pallas kernels, on_device(): pl.pallas_call(window_kernel, out_shape=jax.ShapeDtypeStruct((columns, tr...  28.8 us
    pallas_call x1, Pallas kernels, on_device(): pl.pallas_call(finish_kernel, out_shape=jax.ShapeDtypeStruct((tracers, le...  1.09 us

profile of v2, /device:TPU:710, one launch (start us, length us, event | category | flops | bytes accessed | tf_op | source)
XLA Modules:
  0.0 29.9 jit_solution(105704536690219513)
XLA Ops:
  0.0 28.8 %shard_map.73.source = f32[16,2,64,128]{3,2,1,0:T(8,128)S(1)} custom-call(f32[2,64,16,128]{3,2,1,0:T(8,128)} %bitcast.6, f32[2,64,16,1,128]{4,3,2,1,0:T(1,128)} %bitcast.7, bf16[2,64,16,128]{3,2,1,0:T(8,128)(2,1)} %bitcast.8, f32[2,64]{1,0:T(2,128)} %bitcast.10, f32[64,64]{1,0:T(8,128)} %bitcast.9, f32[1,2]{1,0:T(1,128)} %rate.1, s32[4]{0:T(128)} %block_map.1, ...), custom_call_target="tpu_custom_call" | custom-call | tf_op jit(solution)/shard_map/pallas_call | solution.py:411
  28.8 1.1 %shard_map.74 = f32[2,64,16,1,128]{4,3,2,1,0:T(1,128)} custom-call(f32[16,2,64,128]{3,2,1,0:T(8,128)S(1)} %shard_map.73.source), custom_call_target="tpu_custom_call" | custom-call | tf_op jit(solution)/shard_map/pallas_call | solution.py:468

commit v3 on v2

--- a/solution.py
+++ b/solution.py
@@ -27,10 +27,10 @@
     q0, q1, flow_v, flow_n, half_c, half_d, kappa, diff_v, solve_v, lhs, surf_col,
     rate_s, map_s, ice_s,
     own_surf, other_surf, own_late, other_late, west_surf, weights, increment,
-    halo_e, west_out, west_in, west_row, ring_out, ring_in,
+    halo_e, west_out, west_in, west_row, ring_out, ring_in, wests, corner_shift,
     mini_out, mini_in, corner_out, corner_n, corner_s,
     pack_out, pack_n, pack_s, pack2_out, pack2_n, pack2_s, flow_p, kappa_p,
-    load_sem, small_sem, send_sem, recv_sem,
+    load_sem, small_sem, send_sem, recv_sem, token,
 ):
     fluid = lax.axis_index("fluid")
     zon = lax.axis_index("zon")
@@ -43,27 +43,26 @@
     north, south = lax.rem(mer + 1, mers), lax.rem(mer + mers - 1, mers)
     across = 1 - fluid
     barrier = pltpu.get_barrier_semaphore()
-    for peer in (
-        (fluid, west, mer),
-        (fluid, west, north),
-        (fluid, west, south),
-        (across, west, mer),
-        (fluid, zon, north),
-        (fluid, zon, south),
-        (across, zon, mer),
-    ):
-        pl.semaphore_signal(barrier, inc=1, device_id=peer, device_id_type=MESH)
+
+    def greet(peers):
+        for peer in peers:
+            pl.semaphore_signal(barrier, inc=1, device_id=peer, device_id_type=MESH)
+
+    before_seam = lax.rem(zon, 24) == 23
+    after_seam = lax.rem(zon, 24) == 0
+    greet(((fluid, west, mer), (fluid, west, north), (fluid, west, south), (across, west, mer)))
+
+    @pl.when(jnp.logical_not(before_seam))
+    def _():
+        greet(((fluid, zon, north), (fluid, zon, south), (across, zon, mer)))
 
     surface = (levels - 1) * (1 - fluid)
     is_atm = fluid == 0
 
+    loads = [pltpu.make_async_copy(rows.at[:, :, x, 0, :], q0.at[x + 1], load_sem.at[x]) for x in range(columns)]
+    loads[last].start()
     flow_load = pltpu.make_async_copy(flow, flow_v, load_sem.at[columns])
     flow_load.start()
-    loads = []
-    for x in range(columns):
-        load = pltpu.make_async_copy(rows.at[:, :, x, 0, :], q0.at[x + 1], load_sem.at[x])
-        load.start()
-        loads.append(load)
     smalls = [
         pltpu.make_async_copy(block_map, map_s, small_sem.at[0]),
         pltpu.make_async_copy(ice_mask, ice_s, small_sem.at[1]),
@@ -74,8 +73,8 @@
     ]
     for copy in smalls:
         copy.start()
-
-    sent = []
+    for x in (last - 1, *range(last - 1)):
+        loads[x].start()
 
     def copy_to(slot, peer, source, target):
         return pltpu.make_async_remote_copy(
@@ -106,7 +105,14 @@
     def send(*copies):
         for copy in copies:
             copy.start()
-            sent.append(copy)
+
+    def send_before_seam(*copies):
+        pl.when(before_seam)(lambda: send(*copies))
+
+    @pl.when(before_seam)
+    def _():
+        pl.semaphore_wait(barrier, 4)
+        send(surf_w)
 
     lane = lax.broadcasted_iota(jnp.int32, (levels, 128), 1)
     lane32 = lax.broadcasted_iota(jnp.int32, (32, 128), 1)
@@ -144,6 +150,14 @@
 
     def at_edges(sides, j):
         return pltpu.roll(sides, (127 - 2 * j) % 128, 1)
+
+    loads[last].wait()
+    west_out[...] = q0[columns].astype(BF16)
+    total = jnp.zeros((32, 128), F32)
+    for t in range(2):
+        total = packed_lanes(q0[columns, t], 2 * last + t, total)
+    corner_out[...] = mini(total)
+    send_before_seam(corner_to_n, corner_to_s, row_w)
 
     for copy in smalls:
         copy.wait()
@@ -171,22 +185,6 @@
         field[0] = zero_block
         field[columns + 1] = zero_block
 
-    flow_load.wait()
-    for piece, half in ((0, half_c), (1, half_d)):
-        flow_n[piece] = flow_v[piece].astype(F32).reshape(levels * columns, 128) * 0.5
-        for x in range(columns):
-            half[x] = flow_n[piece, pl.ds(x, levels, stride=columns), :]
-    total = jnp.zeros((32, 128), F32)
-    for x in range(columns):
-        block = half_d[x]
-        for t in range(2):
-            total = packed_lanes(block, 2 * x + t, total)
-    flow_p[...] = total
-    mini_out[...] = mini(total)
-    ring_out[0] = half_c[last].astype(BF16)
-    for load in loads:
-        load.wait()
-
     def solve_of(value):
         return jnp.dot(lhs[...], stacked(value), preferred_element_type=F32)
 
@@ -208,19 +206,42 @@
         target[x + offset, 0] = solved[:, :128]
         target[x + offset, 1] = solved[:, 128:]
 
+    flow_load.wait()
+    for piece in range(2):
+        flow_n[piece] = flow_v[piece].astype(F32).reshape(levels * columns, 128) * 0.5
+
+    def turn(x):
+        half_c[x] = flow_n[0, pl.ds(x, levels, stride=columns), :]
+        half_d[x] = flow_n[1, pl.ds(x, levels, stride=columns), :]
+
+    turn(last)
+    total = jnp.zeros((32, 128), F32)
+    for t in range(2):
+        total = packed_lanes(half_d[last], 2 * last + t, total)
+    mini_out[...] = mini(total)
+    loads[last - 1].wait()
     interior(q0, q1, 1, last)
+    ring_out[0] = half_c[last].astype(BF16)
     ring_out[1:3] = q1[columns].astype(BF16)
-    west_out[...] = q0[columns].astype(BF16)
-    total = pack(q0)
-    pack_out[0:32] = total
-    corner_out[...] = mini(total)
+    send_before_seam(ring, mini_w)
+
+    for x in range(last):
+        turn(x)
+        for t in range(2):
+            total = packed_lanes(half_d[x], 2 * x + t, total)
+    flow_p[...] = total
+    for x in range(last - 1):
+        loads[x].wait()
+    pack_out[0:32] = pack(q0)
     ends = jnp.zeros((32, 128), F32)
     for t in range(2):
         ends = packed_lanes(half_c[0], 2 * last + t, ends)
     pack_out[32:40] = mini(ends)
 
-    pl.semaphore_wait(barrier, 7)
-    send(row_w, ring, mini_w, corner_to_n, corner_to_s, surf_w, surf_0, pack_to_n, pack_to_s)
+    @pl.when(jnp.logical_not(before_seam))
+    def _():
+        pl.semaphore_wait(barrier, 7)
+        send(corner_to_n, corner_to_s, row_w, ring, mini_w, surf_w, surf_0, pack_to_n, pack_to_s)
 
     block_of = lax.broadcasted_iota(jnp.int32, (8, 128), 1) // 32
     base = 4 * mer
@@ -260,13 +281,16 @@
     def side_terms(beyond, half):
         return (kappa_p[...] + jnp.where(even, -half, half)) * beyond
 
-    def greet_west():
+    @pl.when(jnp.logical_not(after_seam))
+    def _():
         row_w.wait_recv()
         row_e.start()
 
-    sent.append(row_e)
-    seam = lax.rem(zon, 24) == 0
-    pl.when(jnp.logical_not(seam))(greet_west)
+    @pl.when(before_seam)
+    def _():
+        row_e.wait_recv()
+        pl.semaphore_wait(token, 1)
+        send(surf_0, pack_to_n, pack_to_s)
 
     surf_0.wait_recv()
     increments(0)
@@ -290,7 +314,7 @@
 
     for x in range(last):
         keep(x, corrected(0, q1, 1, x))
-    row_e.wait_recv()
+    pl.when(jnp.logical_not(before_seam))(row_e.wait_recv)
     k_c = [kappa[t] - half_c[last] for t in range(2)]
     solved = solve_of(jnp.concatenate([k_c[t] * halo_e[0, t] for t in range(2)], axis=1))
     values = corrected(0, q1, 1, last)
@@ -299,11 +323,64 @@
     pack2_out[...] = pack(q1)
     send(pack2_to_n, pack2_to_s)
 
+    def west_side(late):
+        if late:
+            row_w.wait_recv()
+            corner_to_n.wait_recv()
+            surf_w.wait_recv()
+            row_e.start()
+            pl.semaphore_signal(token, inc=1, device_id=(fluid, west, south), device_id_type=MESH)
+        west_row[...] = west_in[...].astype(F32)
+        solved = solve_of(jnp.concatenate([(kappa[t] + half_c[0]) * west_row[t] for t in range(2)], axis=1))
+        for t in range(2):
+            q1[1, t] = q1[1, t] + solved[:, 128 * t : 128 * t + 128]
+            own_late[t : t + 1, :] = q1[1, t, pl.ds(surface, 1), :]
+        send(surf_late, row2_e)
+        ring.wait_recv()
+        k_w = [kappa[t] - ring_in[0].astype(F32) for t in range(2)]
+        own = solve_of(jnp.concatenate([k_w[t] * q0[1, t] for t in range(2)], axis=1))
+        if not late:
+            surf_w.wait_recv()
+        west_own = jnp.concatenate([west_row[t, pl.ds(surface, 1), :] for t in range(2)], axis=0)
+        west_flux = exchange(west_own, west_surf[...], 0) * rates
+        for t in range(2):
+            wests[t] = (
+                ring_in[1 + t].astype(F32) + own[:, 128 * t : 128 * t + 128] + column * west_flux[t : t + 1]
+            )
+
+    def west_corners(late):
+        mini_w.wait_recv()
+        if not late:
+            corner_to_n.wait_recv()
+        corner_to_s.wait_recv()
+        from_n = from_mini(corner_n[...])
+        from_s = from_mini(corner_s[...])
+        corners = side_terms(near(from_n, from_s), from_mini(mini_in[...]))
+        mixed = jnp.where(
+            even,
+            (kappa_p[...] + from_mini(pack_s[32:40])) * from_s * has_south,
+            (kappa_p[...] + from_mini(pack_n[32:40])) * from_n * has_north,
+        )
+        solved = solve_of(jnp.concatenate([unpacked(corners), unpacked(mixed)], axis=1))
+        for t in range(2):
+            wests[t] = wests[t] + jnp.where(edge, at_edges(solved[:, 0:128], 2 * last + t), 0.0)
+        mixed = solved[:, 128:256]
+        corner_shift[...] = jnp.where((lane & 1) == 0, pltpu.roll(mixed, 67, 1), pltpu.roll(mixed, 69, 1))
+
+    tracer = lax.broadcasted_iota(jnp.int32, (2, 128), 0)
+    rates = jnp.where(tracer == 0, rate_s[0, 0], rate_s[0, 1])
+
+    @pl.when(jnp.logical_not(after_seam))
+    def _():
+        west_side(False)
+        west_corners(False)
+
     def second_body(x, carry):
         interior(q1, res, 0, x)
         return carry
 
     lax.fori_loop(2, columns, second_body, 0, unroll=2)
+    pl.when(after_seam)(lambda: west_side(True))
     surf_1.wait_recv()
     increments(1)
     pack2_to_n.wait_recv()
@@ -316,50 +393,9 @@
             res[x, t] = values[t]
     beyond = unpacked(beyond)
 
-    pl.when(seam)(greet_west)
-    ring.wait_recv()
-    mini_w.wait_recv()
-    corner_to_n.wait_recv()
-    corner_to_s.wait_recv()
-    west_row[...] = west_in[...].astype(F32)
-    k_c = [kappa[t] + half_c[0] for t in range(2)]
-    k_w = [kappa[t] - ring_in[0].astype(F32) for t in range(2)]
-    from_n = from_mini(corner_n[...])
-    from_s = from_mini(corner_s[...])
-    corners = side_terms(near(from_n, from_s), from_mini(mini_in[...]))
-    mixed = jnp.where(
-        even,
-        (kappa_p[...] + from_mini(pack_s[32:40])) * from_s * has_south,
-        (kappa_p[...] + from_mini(pack_n[32:40])) * from_n * has_north,
-    )
-    solved = solve_of(
-        jnp.concatenate(
-            [k_c[t] * west_row[t] for t in range(2)]
-            + [k_w[t] * q0[1, t] for t in range(2)]
-            + [unpacked(corners), unpacked(mixed)],
-            axis=1,
-        )
-    )
-    pieces = [solved[:, 128 * i : 128 * i + 128] for i in range(6)]
-    firsts = [q1[1, t] + pieces[t] for t in range(2)]
-    for t in range(2):
-        q1[1, t] = firsts[t]
-        own_late[t : t + 1, :] = q1[1, t, pl.ds(surface, 1), :]
-    send(surf_late, row2_e)
-    shift = jnp.where((lane & 1) == 0, pltpu.roll(pieces[5], 67, 1), pltpu.roll(pieces[5], 69, 1))
-    beyond_first = beyond + shift
-    tracer = lax.broadcasted_iota(jnp.int32, (2, 128), 0)
-    rates = jnp.where(tracer == 0, rate_s[0, 0], rate_s[0, 1])
-    surf_w.wait_recv()
-    west_own = jnp.concatenate([west_row[t, pl.ds(surface, 1), :] for t in range(2)], axis=0)
-    west_flux = exchange(west_own, west_surf[...], 0) * rates
-    wests = [
-        ring_in[1 + t].astype(F32)
-        + pieces[2 + t]
-        + column * west_flux[t : t + 1]
-        + jnp.where(edge, at_edges(pieces[4], 2 * last + t), 0.0)
-        for t in range(2)
-    ]
+    pl.when(after_seam)(lambda: west_corners(True))
+    firsts = [q1[1, t] for t in range(2)]
+    beyond_first = beyond + corner_shift[...]
 
     def full(k, c, d, q, to_east, to_west, around):
         return (
@@ -389,7 +425,10 @@
     )
     for t in range(2):
         res[last, t] = res[last, t] + solved[:, 128 * t : 128 * t + 128]
-    for copy in sent:
+    for copy in (
+        row_w, surf_w, surf_0, corner_to_n, corner_to_s, ring, mini_w, pack_to_n,
+        pack_to_s, row_e, surf_1, pack2_to_n, pack2_to_s, surf_late, row2_e,
+    ):
         copy.wait_send()
 
 
@@ -441,6 +480,8 @@
             vmem((tracers, levels, merid), F32),
             vmem((tracers + 1, levels, merid), BF16),
             vmem((tracers + 1, levels, merid), BF16),
+            vmem((tracers, levels, merid), F32),
+            vmem((levels, merid), F32),
         ]
         + [vmem((8, merid), F32)] * 5
         + [vmem((40, merid), F32)] * 3
@@ -450,6 +491,7 @@
             dma((6,)),
             dma((15,)),
             dma((15,)),
+            pltpu.SemaphoreType.REGULAR,
         ],
         compiler_params=pltpu.CompilerParams(
             collective_id=0, has_side_effects=True, vmem_limit_bytes=48 * 2**20

time: 30.1 us -> 27 us (0.90)
  the two profiles are of different devices: /device:TPU:710 before, /device:TPU:1 now
where the time goes in v3:
time: 27 us; the launch traced here: 26.7 us
  Pallas kernels  26.7 us (99%)
    pallas_call x1, Pallas kernels, on_device(): pl.pallas_call(window_kernel, out_shape=jax.ShapeDtypeStruct((columns, tr...  25.6 us
    pallas_call x1, Pallas kernels, on_device(): pl.pallas_call(finish_kernel, out_shape=jax.ShapeDtypeStruct((tracers, le...  1.09 us

profile of v3, /device:TPU:1, one launch (start us, length us, event | category | flops | bytes accessed | tf_op | source)
XLA Modules:
  0.0 26.7 jit_solution(288060881425645795)
XLA Ops:
  0.0 25.6 %shard_map.73.source = f32[16,2,64,128]{3,2,1,0:T(8,128)S(1)} custom-call(f32[2,64,16,128]{3,2,1,0:T(8,128)} %bitcast.6, f32[2,64,16,1,128]{4,3,2,1,0:T(1,128)} %bitcast.7, bf16[2,64,16,128]{3,2,1,0:T(8,128)(2,1)} %bitcast.8, f32[2,64]{1,0:T(2,128)} %bitcast.10, f32[64,64]{1,0:T(8,128)} %bitcast.9, f32[1,2]{1,0:T(1,128)} %rate.1, s32[4]{0:T(128)} %block_map.1, ...), custom_call_target="tpu_custom_call" | custom-call | tf_op jit(solution)/shard_map/pallas_call | solution.py:450
  25.6 1.1 %shard_map.74 = f32[2,64,16,1,128]{4,3,2,1,0:T(1,128)} custom-call(f32[16,2,64,128]{3,2,1,0:T(8,128)S(1)} %shard_map.73.source), custom_call_target="tpu_custom_call" | custom-call | tf_op jit(solution)/shard_map/pallas_call | solution.py:510

commit v4 on v3

--- a/solution.py
+++ b/solution.py
@@ -30,7 +30,7 @@
     halo_e, west_out, west_in, west_row, ring_out, ring_in, wests, corner_shift,
     mini_out, mini_in, corner_out, corner_n, corner_s,
     pack_out, pack_n, pack_s, pack2_out, pack2_n, pack2_s, flow_p, kappa_p,
-    load_sem, small_sem, send_sem, recv_sem, token,
+    load_sem, small_sem, send_sem, recv_sem, hello, token,
 ):
     fluid = lax.axis_index("fluid")
     zon = lax.axis_index("zon")
@@ -112,6 +112,8 @@
     @pl.when(before_seam)
     def _():
         pl.semaphore_wait(barrier, 4)
+        for peer in ((fluid, east, mer), (fluid, east, north), (across, east, mer)):
+            pl.semaphore_signal(hello, inc=1, device_id=peer, device_id_type=MESH)
         send(surf_w)
 
     lane = lax.broadcasted_iota(jnp.int32, (levels, 128), 1)
@@ -288,8 +290,7 @@
 
     @pl.when(before_seam)
     def _():
-        row_e.wait_recv()
-        pl.semaphore_wait(token, 1)
+        pl.semaphore_wait(token, 2)
         send(surf_0, pack_to_n, pack_to_s)
 
     surf_0.wait_recv()
@@ -314,7 +315,7 @@
 
     for x in range(last):
         keep(x, corrected(0, q1, 1, x))
-    pl.when(jnp.logical_not(before_seam))(row_e.wait_recv)
+    row_e.wait_recv()
     k_c = [kappa[t] - half_c[last] for t in range(2)]
     solved = solve_of(jnp.concatenate([k_c[t] * halo_e[0, t] for t in range(2)], axis=1))
     values = corrected(0, q1, 1, last)
@@ -325,11 +326,11 @@
 
     def west_side(late):
         if late:
+            pl.semaphore_wait(hello, 3)
+            for peer in ((fluid, west, mer), (fluid, west, south)):
+                pl.semaphore_signal(token, inc=1, device_id=peer, device_id_type=MESH)
+            row_e.start()
             row_w.wait_recv()
-            corner_to_n.wait_recv()
-            surf_w.wait_recv()
-            row_e.start()
-            pl.semaphore_signal(token, inc=1, device_id=(fluid, west, south), device_id_type=MESH)
         west_row[...] = west_in[...].astype(F32)
         solved = solve_of(jnp.concatenate([(kappa[t] + half_c[0]) * west_row[t] for t in range(2)], axis=1))
         for t in range(2):
@@ -339,8 +340,7 @@
         ring.wait_recv()
         k_w = [kappa[t] - ring_in[0].astype(F32) for t in range(2)]
         own = solve_of(jnp.concatenate([k_w[t] * q0[1, t] for t in range(2)], axis=1))
-        if not late:
-            surf_w.wait_recv()
+        surf_w.wait_recv()
         west_own = jnp.concatenate([west_row[t, pl.ds(surface, 1), :] for t in range(2)], axis=0)
         west_flux = exchange(west_own, west_surf[...], 0) * rates
         for t in range(2):
@@ -348,10 +348,9 @@
                 ring_in[1 + t].astype(F32) + own[:, 128 * t : 128 * t + 128] + column * west_flux[t : t + 1]
             )
 
-    def west_corners(late):
+    def west_corners():
         mini_w.wait_recv()
-        if not late:
-            corner_to_n.wait_recv()
+        corner_to_n.wait_recv()
         corner_to_s.wait_recv()
         from_n = from_mini(corner_n[...])
         from_s = from_mini(corner_s[...])
@@ -373,7 +372,7 @@
     @pl.when(jnp.logical_not(after_seam))
     def _():
         west_side(False)
-        west_corners(False)
+        west_corners()
 
     def second_body(x, carry):
         interior(q1, res, 0, x)
@@ -393,7 +392,13 @@
             res[x, t] = values[t]
     beyond = unpacked(beyond)
 
-    pl.when(after_seam)(lambda: west_corners(True))
+    row2_e.wait_recv()
+    solved = solve_of(
+        jnp.concatenate([(kappa[t] - half_c[last]) * halo_e[1, t] for t in range(2)], axis=1)
+    )
+    for t in range(2):
+        res[last, t] = res[last, t] + solved[:, 128 * t : 128 * t + 128]
+    pl.when(after_seam)(west_corners)
     firsts = [q1[1, t] for t in range(2)]
     beyond_first = beyond + corner_shift[...]
 
@@ -419,12 +424,6 @@
     for t in range(2):
         res[0, t] = solved[:, 128 * t : 128 * t + 128] + column * late_flux[t : t + 1]
 
-    row2_e.wait_recv()
-    solved = solve_of(
-        jnp.concatenate([(kappa[t] - half_c[last]) * halo_e[1, t] for t in range(2)], axis=1)
-    )
-    for t in range(2):
-        res[last, t] = res[last, t] + solved[:, 128 * t : 128 * t + 128]
     for copy in (
         row_w, surf_w, surf_0, corner_to_n, corner_to_s, ring, mini_w, pack_to_n,
         pack_to_s, row_e, surf_1, pack2_to_n, pack2_to_s, surf_late, row2_e,
@@ -492,6 +491,7 @@
             dma((15,)),
             dma((15,)),
             pltpu.SemaphoreType.REGULAR,
+            pltpu.SemaphoreType.REGULAR,
         ],
         compiler_params=pltpu.CompilerParams(
             collective_id=0, has_side_effects=True, vmem_limit_bytes=48 * 2**20

time: 27 us -> 26.7 us (0.989)
  no operation moved by 1% of the time
where the time goes in v4:
time: 26.7 us; the launch traced here: 26.5 us
  Pallas kernels  26.5 us (99%)
    pallas_call x1, Pallas kernels, on_device(): pl.pallas_call(window_kernel, out_shape=jax.ShapeDtypeStruct((columns, tr...  25.4 us
    pallas_call x1, Pallas kernels, on_device(): pl.pallas_call(finish_kernel, out_shape=jax.ShapeDtypeStruct((tracers, le...  1.09 us

profile of v4, /device:TPU:1, one launch (start us, length us, event | category | flops | bytes accessed | tf_op | source)
XLA Modules:
  0.0 26.5 jit_solution(17177541411569828794)
XLA Ops:
  0.0 25.4 %shard_map.73.source = f32[16,2,64,128]{3,2,1,0:T(8,128)S(1)} custom-call(f32[2,64,16,128]{3,2,1,0:T(8,128)} %bitcast.6, f32[2,64,16,1,128]{4,3,2,1,0:T(1,128)} %bitcast.7, bf16[2,64,16,128]{3,2,1,0:T(8,128)(2,1)} %bitcast.8, f32[2,64]{1,0:T(2,128)} %bitcast.10, f32[64,64]{1,0:T(8,128)} %bitcast.9, f32[1,2]{1,0:T(1,128)} %rate.1, s32[4]{0:T(128)} %block_map.1, ...), custom_call_target="tpu_custom_call" | custom-call | tf_op jit(solution)/shard_map/pallas_call | solution.py:449
  25.5 1.1 %shard_map.74 = f32[2,64,16,1,128]{4,3,2,1,0:T(1,128)} custom-call(f32[16,2,64,128]{3,2,1,0:T(8,128)S(1)} %shard_map.73.source), custom_call_target="tpu_custom_call" | custom-call | tf_op jit(solution)/shard_map/pallas_call | solution.py:510

commit v5 on v4

--- a/solution.py
+++ b/solution.py
@@ -155,11 +155,12 @@
 
     loads[last].wait()
     west_out[...] = q0[columns].astype(BF16)
+    send_before_seam(row_w)
     total = jnp.zeros((32, 128), F32)
     for t in range(2):
         total = packed_lanes(q0[columns, t], 2 * last + t, total)
     corner_out[...] = mini(total)
-    send_before_seam(corner_to_n, corner_to_s, row_w)
+    send_before_seam(corner_to_n, corner_to_s)
 
     for copy in smalls:
         copy.wait()

time: 26.7 us -> 26.6 us (level)
  no operation moved by 1% of the time
where the time goes in v5:
time: 26.6 us; the launch traced here: 26.5 us
  Pallas kernels  26.5 us (100%)
    pallas_call x1, Pallas kernels, on_device(): pl.pallas_call(window_kernel, out_shape=jax.ShapeDtypeStruct((columns, tr...  25.4 us
    pallas_call x1, Pallas kernels, on_device(): pl.pallas_call(finish_kernel, out_shape=jax.ShapeDtypeStruct((tracers, le...  1.09 us

profile of v5, /device:TPU:1, one launch (start us, length us, event | category | flops | bytes accessed | tf_op | source)
XLA Modules:
  0.0 26.5 jit_solution(12863481997010245868)
XLA Ops:
  0.0 25.4 %shard_map.73.source = f32[16,2,64,128]{3,2,1,0:T(8,128)S(1)} custom-call(f32[2,64,16,128]{3,2,1,0:T(8,128)} %bitcast.6, f32[2,64,16,1,128]{4,3,2,1,0:T(1,128)} %bitcast.7, bf16[2,64,16,128]{3,2,1,0:T(8,128)(2,1)} %bitcast.8, f32[2,64]{1,0:T(2,128)} %bitcast.10, f32[64,64]{1,0:T(8,128)} %bitcast.9, f32[1,2]{1,0:T(1,128)} %rate.1, s32[4]{0:T(128)} %block_map.1, ...), custom_call_target="tpu_custom_call" | custom-call | tf_op jit(solution)/shard_map/pallas_call | solution.py:450
  25.4 1.1 %shard_map.74 = f32[2,64,16,1,128]{4,3,2,1,0:T(1,128)} custom-call(f32[16,2,64,128]{3,2,1,0:T(8,128)S(1)} %shard_map.73.source), custom_call_target="tpu_custom_call" | custom-call | tf_op jit(solution)/shard_map/pallas_call | solution.py:511
